TPU v7x, 256 devices: a whole 4x4x8 slice. The times are simulated.
256 devices in a mesh: dp: 64 (over y, z, core), rep: 4 (over x).
Axes of the slice: x: 4, y: 4, z: 8, core: 2. Of those that a mesh axis runs over, the one named last changes fastest.
Arguments:
- item_table: bfloat16 [32768, 512], P(('dp', 'rep')), may hold values from -6 to 6
- requests: int32 [256, 256, 2], P(('dp', 'rep')), may hold values from 0 to 127, as said below
- event_slot: int32 [131072], P(('dp', 'rep')), may hold values from 0 to 511, as said below
- lengths: int32 [256, 4], P(('dp', 'rep')), may hold values from 1 to 256, 512 in all within a row
- leaf_ids: int32 [131072, 8], P(('dp', 'rep')), may hold values from 0 to 31
- leaf_table: bfloat16 [256, 512], replicated, may hold values from -2.09375 to 2.09375
- w_in: bfloat16 [512, 2048], replicated, may hold values from -0.25 to 0.25
- w_out: bfloat16 [512, 512], replicated, may hold values from -0.25 to 0.25
- cotangent: bfloat16 [131072, 512], P(('dp', 'rep')), may hold values from -6 to 6
Outputs:
- output: bfloat16 [131072, 512], P(('dp', 'rep'))
- table_grad: float32 [32768, 512], P(('dp', 'rep'))
- leaf_grad: float32 [256, 512], replicated
- w_in_grad: float32 [512, 2048], replicated
- w_out_grad: float32 [512, 512], replicated
Inputs may be any that keep to these rules, and one draw needn't show every extreme that they name: `requests`: for each device and owner the 2 requested rows are distinct. `event_slot`: every one of a device's 512 slots is named by at least one of its events.
All inputs are finite; a program needn't handle non-finite values.
Results may differ from a plain program's by a relative error of at most 0.014.
Values may be sent and summed in bfloat16 or wider, within the bound.
A program may use at most 64 MiB of HBM per device.

v0:
```python
import jax
import jax.numpy as jnp
from jax import lax
from jax.sharding import PartitionSpec as P

HEADS = 4
epsilon = 1e-06


def normalize(values):
    center = values - jnp.mean(values, axis=-1, keepdims=True)
    spread = jnp.mean(center * center, axis=-1, keepdims=True)
    return center * lax.rsqrt(spread + epsilon)


def visible(lengths, count):
    ends = jnp.cumsum(lengths)
    places = jnp.arange(count, dtype=jnp.int32)
    segment = jnp.sum((places[:, None] >= ends[None, :]).astype(jnp.int32), axis=1)
    same = segment[:, None] == segment[None, :]
    return jnp.logical_and(same, places[None, :] <= places[:, None])


def front(rows, event_slot, lengths, leaf_ids, leaf_table, w_in):
    count = event_slot.shape[0]
    picker = (event_slot[:, None] == jnp.arange(rows.shape[0], dtype=jnp.int32)[None, :]).astype(
        jnp.bfloat16
    )
    leaves = leaf_table.shape[0] // leaf_ids.shape[1]
    onehot = (
        (leaf_ids[:, :, None] == jnp.arange(leaves, dtype=jnp.int32)[None, None, :])
        .reshape(count, -1)
        .astype(jnp.bfloat16)
    )
    inputs = (
        jnp.dot(picker, rows, preferred_element_type=jnp.float32)
        + jnp.dot(onehot, leaf_table, preferred_element_type=jnp.float32)
    ).astype(jnp.bfloat16)
    normed = normalize(inputs.astype(jnp.float32)).astype(jnp.bfloat16)
    hidden = jax.nn.silu(jnp.dot(normed, w_in, preferred_element_type=jnp.float32)).astype(
        jnp.bfloat16
    )
    width = w_in.shape[0]
    head_size = width // HEADS
    gates = hidden[:, 0:width]
    value_heads = hidden[:, width : 2 * width].reshape(count, HEADS, head_size)
    query_heads = hidden[:, 2 * width : 3 * width].reshape(count, HEADS, head_size)
    key_heads = hidden[:, 3 * width : 4 * width].reshape(count, HEADS, head_size)
    scores = jnp.einsum(
        "qhd,khd->hqk", query_heads, key_heads, preferred_element_type=jnp.float32
    ) * head_size ** (-0.5)
    allowed = visible(lengths, count)
    weights = jnp.where(allowed[None], jax.nn.silu(scores), 0.0).astype(jnp.bfloat16)
    mixed = jnp.einsum(
        "hqk,khd->qhd", weights, value_heads, preferred_element_type=jnp.float32
    ).reshape(count, width)
    gated = (normalize(mixed) * gates.astype(jnp.float32)).astype(jnp.bfloat16)
    return (inputs, gated)


def back(inputs, gated, w_out):
    return (
        jnp.dot(gated, w_out, preferred_element_type=jnp.float32) + inputs.astype(jnp.float32)
    ).astype(jnp.bfloat16)


def send_asked(wanted):
    result = lax.all_to_all(
        lax.all_to_all(wanted, "dp", split_axis=0, concat_axis=0, tiled=True),
        "rep",
        split_axis=1,
        concat_axis=1,
        tiled=True,
    )
    return result


def send_fetched(fetched):
    result = lax.all_to_all(
        lax.all_to_all(fetched, "dp", split_axis=0, concat_axis=0, tiled=True),
        "rep",
        split_axis=1,
        concat_axis=1,
        tiled=True,
    )
    return result


def send_returned(gradients):
    result = lax.all_to_all(
        lax.all_to_all(gradients, "dp", split_axis=0, concat_axis=0, tiled=True),
        "rep",
        split_axis=1,
        concat_axis=1,
        tiled=True,
    )
    return result


def on_device(
    item_table, requests, event_slot, lengths, leaf_ids, leaf_table, w_in, w_out, cotangent
):
    data_count = lax.axis_size("dp")
    replica_count = lax.axis_size("rep")
    width = item_table.shape[1]
    wanted = requests.reshape(data_count, replica_count, -1)
    asked = send_asked(wanted)
    fetched = item_table[asked]
    arrived = send_fetched(fetched).reshape(-1, width)

    def local_front(rows, table_leaf, weight_in):
        return front(rows, event_slot, lengths[0], leaf_ids, table_leaf, weight_in)

    (inputs, gated), pull_front = jax.vjp(local_front, arrived, leaf_table, w_in)
    output, pull_back = jax.vjp(back, inputs, gated, w_out)
    d_inputs, d_gated, d_out = pull_back(cotangent)
    d_rows, d_leaf, d_in = pull_front((d_inputs, d_gated))
    returned = send_returned(d_rows.reshape(data_count, replica_count, -1, width))
    leaf_sum, in_sum, out_sum = lax.psum(
        (d_leaf.astype(jnp.float32), d_in.astype(jnp.float32), d_out.astype(jnp.float32)),
        ("dp", "rep"),
    )
    table_grad = (
        jnp.zeros(item_table.shape, jnp.float32)
        .at[asked.reshape(-1)]
        .add(returned.reshape(-1, width).astype(jnp.float32))
    )
    share = 1.0 / (data_count * replica_count)
    return (output, table_grad, leaf_sum * share, in_sum * share, out_sum * share)


def solution(mesh):
    return jax.shard_map(
        on_device,
        mesh=mesh,
        in_specs=(
            P(("dp", "rep"), None),
            P(("dp", "rep"), None, None),
            P(("dp", "rep")),
            P(("dp", "rep"), None),
            P(("dp", "rep"), None),
            P(),
            P(),
            P(),
            P(("dp", "rep"), None),
        ),
        out_specs=(P(("dp", "rep"), None), P(("dp", "rep"), None), P(), P(), P()),
        check_vma=False,
    )
```

profile of v0, /device:TPU:97, one launch (start us, length us, event | category | flops | bytes accessed | tf_op | source)
XLA Modules:
  0.0 433.1 jit_solution(8049075674224172676)
XLA Ops:
  7.2 0.9 reshape.199
  8.2 18.3 %all_to_all.30 = s32[64,4,2]{1,2,0:T(2,128)S(1)} all-to-all(s32[64,4,2]{1,2,0:T(2,128)S(1)} %copy.143), channel_id=1, replica_groups=mesh['dp'=64,'rep'=4] {'dp'}, dimensions={0} | all-to-all | bytes 4096 | tf_op jit(solution)/shard_map/all_to_all | solution.py:69
  26.7 7.9 %all_to_all.31 = s32[4,1,128]{2,1,0:T(1,128)S(1)} all-to-all(s32[4,1,128]{2,1,0:T(1,128)S(1)} %reshape.234), channel_id=1, replica_groups=mesh['dp'=64,'rep'=4] {'rep'}, dimensions={0} | all-to-all | bytes 4096 | tf_op jit(solution)/shard_map/all_to_all | solution.py:68
  34.6 0.5 broadcast.167
  35.1 0.7 reduce.3
  36.2 2.9 gather_fusion
  39.1 1.0 reshape.215
  40.1 8.5 %all-to-all-start.2 = ((bf16[64,4,2,512]{3,2,1,0:T(2,128)(2,1)}), bf16[64,4,2,512]{3,2,1,0:T(2,128)(2,1)S(1)}, u32[]{:S(2)}, u32[]{:S(2)}) async-start(bf16[64,4,2,512]{3,2,1,0:T(2,128)(2,1)} %reshape.215), calls=%async_computation.2 | async-start | bytes 1048576 | tf_op jit(solution)/shard_map/all_to_all | solution.py:80
  48.9 1.0 copy.163
  50.1 15.3 %all-to-all-done.2 = bf16[64,4,2,512]{3,2,1,0:T(2,128)(2,1)S(1)} async-done(((bf16[64,4,2,512]{3,2,1,0:T(2,128)(2,1)}), bf16[64,4,2,512]{3,2,1,0:T(2,128)(2,1)S(1)}, u32[]{:S(2)}, u32[]{:S(2)}) %all-to-all-start.2) | async-done | bytes 524320 | tf_op jit(solution)/shard_map/all_to_all | solution.py:80
  65.4 1.2 copy.146
  66.6 3.5 all-to-all-start.3
  70.5 2.3 fusion.42
  72.8 7.3 %all-to-all-done.3 = bf16[64,4,2,512]{3,2,0,1:T(2,128)(2,1)S(1)} async-done(((bf16[64,4,2,512]{3,2,0,1:T(2,128)(2,1)}), bf16[64,4,2,512]{3,2,0,1:T(2,128)(2,1)S(1)}, u32[]{:S(2)}, u32[]{:S(2)}) %all-to-all-start.3) | async-done | bytes 524320 | tf_op jit(solution)/shard_map/all_to_all | solution.py:79
  80.0 1.2 copy.147
  81.2 2.0 reshape.200
  83.2 2.0 convert_reduce_fusion
  85.5 0.5 copy-done.16
  86.0 3.9 multiply_convert_fusion
  89.9 1.3 copy-done.7
  91.2 1.2 slice_bitcast_fusion
  92.4 2.1 copy.176
  94.5 2.0 copy.177
  96.5 4.8 %select_convert_fusion = (bf16[4,512,512]{2,1,0:T(8,128)(2,1)S(1)}, f32[4,512,512]{2,1,0:T(8,128)}) fusion(pred[512,512]{1,0:T(8,128)(4,1)S(1)} %fusion.22, bf16[512,4,128]{0,2,1:T(8,128)(2,1)} %bitcast.68, bf16[512,4,128]{0,2,1:T(8,128)(2,1)} %bitcast.70), kind=kOutput, calls=%fused_computation.11 | convolution fusion | flops 275775488 | bytes 7602176 | tf_op jit(solution)/shard_map/jvp(qhd,khd->hqk)/dot_general | solution.py:49
  101.3 0.8 fusion.41
  102.2 0.9 copy-done.1
  103.1 0.8 fusion.20
  103.9 2.6 copy.171
  106.5 2.1 multiply_reduce_fusion
  108.6 0.7 multiply_multiply_fusion.1
  109.3 3.0 fusion.40
  112.3 0.9 broadcast_add_fusion
  113.2 2.1 copy.172
  115.3 5.1 %fusion.4 = bf16[4,512,512]{2,1,0:T(8,128)(2,1)S(1)} fusion(f32[4,512,512]{2,1,0:T(8,128)} %get-tuple-element.57, pred[512,512]{1,0:T(8,128)(4,1)S(1)} %fusion.22, bf16[4,128,512]{2,1,0:T(8,128)(2,1)} %bitcast.72, bf16[64,4,8,128]{3,2,1,0:T(8,128)(2,1)} %get-tuple-element.46), kind=kOutput, calls=%fused_computation.10 | convolution fusion | flops 283115520 | bytes 7602176 | tf_op jit(solution)/shard_map/transpose(jvp(hqk,khd->qhd))/dot_general | solution.py:54
  120.4 1.2 fusion.45
  121.6 1.6 fusion.44
  123.2 1.5 fusion.43
  124.7 2.1 copy.173
  126.8 2.0 copy.174
  128.8 2.1 copy.175
  130.9 3.6 fusion
  134.5 3.3 fusion.5
  137.8 1.3 fusion.18
  139.5 0.4 fusion.25
  139.9 0.8 copy-done.12
  140.6 1.1 fusion.13
  141.8 1.5 fusion.10
  143.3 2.5 convolution_convert_fusion.1
  145.9 2.0 reshape.212
  147.9 6.8 %all-to-all-start.4 = ((bf16[64,4,2,512]{3,2,1,0:T(2,128)(2,1)}), bf16[64,4,2,512]{3,2,1,0:T(2,128)(2,1)}, u32[]{:S(2)}, u32[]{:S(2)}) async-start(bf16[64,4,2,512]{3,2,1,0:T(2,128)(2,1)} %reshape.212), calls=%async_computation.4 | async-start | bytes 1048576 | tf_op jit(solution)/shard_map/all_to_all | solution.py:91
  155.0 17.6 %all-to-all-done.4 = bf16[64,4,2,512]{3,2,1,0:T(2,128)(2,1)} async-done(((bf16[64,4,2,512]{3,2,1,0:T(2,128)(2,1)}), bf16[64,4,2,512]{3,2,1,0:T(2,128)(2,1)}, u32[]{:S(2)}, u32[]{:S(2)}) %all-to-all-start.4) | async-done | bytes 524320 | tf_op jit(solution)/shard_map/all_to_all | solution.py:91
  172.6 2.2 copy.164
  174.8 4.4 %all-to-all-start.5 = ((bf16[64,4,2,512]{3,2,0,1:T(2,128)(2,1)}), bf16[64,4,2,512]{3,2,0,1:T(2,128)(2,1)}, u32[]{:S(2)}, u32[]{:S(2)}) async-start(bf16[64,4,2,512]{3,2,0,1:T(2,128)(2,1)} %copy.164), calls=%async_computation.5 | async-start | bytes 1048576 | tf_op jit(solution)/shard_map/all_to_all | solution.py:90
  179.2 2.3 fusion.11
  181.6 2.1 copy.167
  183.6 5.3 %all-to-all-done.5 = bf16[64,4,2,512]{3,2,0,1:T(2,128)(2,1)} async-done(((bf16[64,4,2,512]{3,2,0,1:T(2,128)(2,1)}), bf16[64,4,2,512]{3,2,0,1:T(2,128)(2,1)}, u32[]{:S(2)}, u32[]{:S(2)}) %all-to-all-start.5) | async-done | bytes 524320 | tf_op jit(solution)/shard_map/all_to_all | solution.py:90
  188.9 1.2 copy_convert_fusion
  190.1 0.8 copy.166
  191.0 1.7 reshape.226
  192.6 4.9 %scatter_custom_fusion = f32[128,512]{1,0:T(8,128)} fusion(s32[512]{0:T(512)S(1)} %bitcast.79, f32[512,512]{1,0:T(8,128)} %reshape.226, f32[]{:T(128)} %constant.15.clone.1), kind=kCustom, calls=%fused_computation.74 | custom fusion | flops 262144 | bytes 262656 | tf_op jit(solution)/shard_map/scatter-add | solution.py:126
  197.6 221.8 %all-reduce.7.cloned.1.call-done = (f32[256,512]{1,0:T(8,128)}, f32[512,2048]{1,0:T(8,128)}, f32[512,512]{1,0:T(8,128)}) async-done(((f32[256,512]{1,0:T(8,128)}, f32[512,2048]{1,0:T(8,128)}, f32[512,512]{1,0:T(8,128)}), (f32[256,512]{1,0:T(8,128)}, f32[512,2048]{1,0:T(8,128)}, f32[512,512]{1,0:T(8,128)})) %all-reduce.7.cloned.1.call-update) | async-done | bytes 5767184 | tf_op jit(solution)/shard_map/psum | solution.py:119
  419.4 4.9 %broadcast_multiply_fusion = f32[512,2048]{1,0:T(8,128)} fusion(f32[512,2048]{1,0:T(8,128)} %get-tuple-element.41), kind=kLoop, calls=%fused_computation.17 | loop fusion | flops 1048576 | bytes 8388608 | tf_op jit(solution)/shard_map/mul | solution.py:129
  424.3 1.1 broadcast_multiply_fusion.1
  425.4 0.8 broadcast_multiply_fusion.2
  (67 shorter events, 2.4 us)
Async XLA Ops:
  7.2 78.8 %copy-start = (bf16[512,2048]{1,0:T(8,128)(2,1)S(1)}, bf16[512,2048]{1,0:T(8,128)(2,1)}, u32[]{:S(2)}) copy-start(bf16[512,2048]{1,0:T(8,128)(2,1)} %param.15) | copy-start | bytes 6291460
  7.2 41.5 %copy-start.21 = (s32[1,4]{1,0:T(1,128)S(1)}, s32[1,4]{1,0:T(1,128)}, u32[]{:S(2)}) copy-start(s32[1,4]{1,0:T(1,128)} %param.12) | copy-start | bytes 52
  7.2 41.7 %copy-start.4 = (bf16[512,512]{1,0:T(8,128)(2,1)S(1)}, bf16[512,512]{1,0:T(8,128)(2,1)}, u32[]{:S(2)}) copy-start(bf16[512,512]{1,0:T(8,128)(2,1)} %param.17) | copy-start | bytes 1572868
  26.5 23.4 %copy-start.18 = (s32[512,8]{0,1:T(8,128)S(1)}, s32[512,8]{0,1:T(8,128)}, u32[]{:S(2)}) copy-start(s32[512,8]{0,1:T(8,128)} %param.13) | copy-start | bytes 49156
  40.1 43.1 %copy-start.19 = (s32[512]{0:T(512)S(1)}, s32[512]{0:T(512)}, u32[]{:S(2)}) copy-start(s32[512]{0:T(512)} %param.11) | copy-start | bytes 6148
  40.1 25.3 %all-to-all-start.2 = ((bf16[64,4,2,512]{3,2,1,0:T(2,128)(2,1)}), bf16[64,4,2,512]{3,2,1,0:T(2,128)(2,1)S(1)}, u32[]{:S(2)}, u32[]{:S(2)}) async-start(bf16[64,4,2,512]{3,2,1,0:T(2,128)(2,1)} %reshape.215), calls=%async_computation.2 | async-start | bytes 1048576 | tf_op jit(solution)/shard_map/all_to_all | solution.py:80
  66.6 13.5 %all-to-all-start.3 = ((bf16[64,4,2,512]{3,2,0,1:T(2,128)(2,1)}), bf16[64,4,2,512]{3,2,0,1:T(2,128)(2,1)S(1)}, u32[]{:S(2)}, u32[]{:S(2)}) async-start(bf16[64,4,2,512]{3,2,0,1:T(2,128)(2,1)} %copy.146), calls=%async_computation.3 | async-start | bytes 1048576 | tf_op jit(solution)/shard_map/all_to_all | solution.py:79
  70.0 349.4 %all-reduce.7.cloned.1.call-start = ((), (), s32[]{:S(2)}) async-start(), calls=%async_computation.6 | async-start | bytes 11534336 | tf_op jit(solution)/shard_map/psum | solution.py:119
  85.5 0.5 copy-start.16
  89.9 1.4 copy-start.7
  96.5 4.9 %copy-start.8 = (bf16[64,4,8,128]{3,2,1,0:T(8,128)(2,1)S(1)}, bf16[64,4,8,128]{3,2,1,0:T(8,128)(2,1)}, u32[]{:S(2)}) copy-start(bf16[64,4,8,128]{3,2,1,0:T(8,128)(2,1)} %get-tuple-element.46) | copy-start | bytes 1572868
  101.3 2.6 copy-start.2
  102.2 1.0 copy-start.1
  115.3 5.1 %copy-start.10 = (bf16[512,512]{0,1:T(8,128)(2,1)S(1)}, bf16[512,512]{0,1:T(8,128)(2,1)}, u32[]{:S(2)}) copy-start(bf16[512,512]{0,1:T(8,128)(2,1)} %copy.176) | copy-start | bytes 1572868
  115.3 6.3 %copy-start.11 = (bf16[512,512]{0,1:T(8,128)(2,1)S(1)}, bf16[512,512]{0,1:T(8,128)(2,1)}, u32[]{:S(2)}) copy-start(bf16[512,512]{0,1:T(8,128)(2,1)} %copy.177) | copy-start | bytes 1572868
  120.4 2.9 copy-start.3
  120.4 2.9 copy-start.13
  137.8 1.3 copy-start.17
  137.8 1.6 copy-start.9
  137.8 4.0 copy-start.5
  139.8 0.8 copy-start.12
  141.8 1.5 copy-start.20
  143.3 35.9 %copy-start.6 = (bf16[512,512]{1,0:T(8,128)(2,1)S(1)}, bf16[512,512]{1,0:T(8,128)(2,1)}, u32[]{:S(2)}) copy-start(bf16[512,512]{1,0:T(8,128)(2,1)} %get-tuple-element.45) | copy-start | bytes 1572868
  147.9 24.7 %all-to-all-start.4 = ((bf16[64,4,2,512]{3,2,1,0:T(2,128)(2,1)}), bf16[64,4,2,512]{3,2,1,0:T(2,128)(2,1)}, u32[]{:S(2)}, u32[]{:S(2)}) async-start(bf16[64,4,2,512]{3,2,1,0:T(2,128)(2,1)} %reshape.212), calls=%async_computation.4 | async-start | bytes 1048576 | tf_op jit(solution)/shard_map/all_to_all | solution.py:91
  174.8 14.1 %all-to-all-start.5 = ((bf16[64,4,2,512]{3,2,0,1:T(2,128)(2,1)}), bf16[64,4,2,512]{3,2,0,1:T(2,128)(2,1)}, u32[]{:S(2)}, u32[]{:S(2)}) async-start(bf16[64,4,2,512]{3,2,0,1:T(2,128)(2,1)} %copy.164), calls=%async_computation.5 | async-start | bytes 1048576 | tf_op jit(solution)/shard_map/all_to_all | solution.py:90
  419.4 4.9 %copy-start.14 = (f32[512,512]{1,0:T(8,128)S(1)}, f32[512,512]{1,0:T(8,128)}, u32[]{:S(2)}) copy-start(f32[512,512]{1,0:T(8,128)} %get-tuple-element.42) | copy-start | bytes 3145732
  419.4 6.0 %copy-start.15 = (f32[256,512]{1,0:T(8,128)S(1)}, f32[256,512]{1,0:T(8,128)}, u32[]{:S(2)}) copy-start(f32[256,512]{1,0:T(8,128)} %get-tuple-element.40) | copy-start | bytes 1572868
Sparse Core Ops, SparseCore 0:
  143.4 275.9 all-reduce.6
where the time goes:
time: 434 us; the launch traced here: 433 us
  waiting for transfers between devices  267 us (62%)
  local copies, waits for them, and re-layouts  40.3 us (9%)
  matrix products  37.4 us (9%)
  blocking collectives  26.2 us (6%)
  other arithmetic  24 us (6%)
  starting transfers between devices  23.4 us (5%)
  between operations  14.4 us (3%)
    psum x1, waiting for transfers between devices, on_device(): lax.psum((d_leaf.astype(jnp.float32), d_in.astype(jnp.float32), d_out.ast...  222 us
    all_to_all x1, blocking collectives, send_asked(): lax.all_to_all(wanted, 'dp', split_axis=0, concat_axis=0, tiled=True)  18.3 us
    all_to_all x1, waiting for transfers between devices, send_returned(): lax.all_to_all(gradients, 'dp', split_axis=0, concat_axis=0, tiled=True)  17.6 us
    all_to_all x1, waiting for transfers between devices, send_fetched(): lax.all_to_all(fetched, 'dp', split_axis=0, concat_axis=0, tiled=True)  15.3 us
  transfers between devices with their start and end apart: 5, of which 5 were waited for; matrix products, arithmetic and copies ran while one was open for 6% of the time, Pallas kernels for 0%

commit v1 on v0

--- a/solution.py
+++ b/solution.py
@@ -116,9 +116,16 @@
     d_inputs, d_gated, d_out = pull_back(cotangent)
     d_rows, d_leaf, d_in = pull_front((d_inputs, d_gated))
     returned = send_returned(d_rows.reshape(data_count, replica_count, -1, width))
-    leaf_sum, in_sum, out_sum = lax.psum(
-        (d_leaf.astype(jnp.float32), d_in.astype(jnp.float32), d_out.astype(jnp.float32)),
-        ("dp", "rep"),
+
+    def create_columns_here(arr_in):
+        ax_name = "dp"
+        across = "rep"
+        for no in (across, ax_name):
+            arr_in = lax.psum(arr_in, no)
+        return arr_in
+
+    leaf_sum, in_sum, out_sum = create_columns_here(
+        (d_leaf.astype(jnp.float32), d_in.astype(jnp.float32), d_out.astype(jnp.float32))
     )
     table_grad = (
         jnp.zeros(item_table.shape, jnp.float32)

time: 434 us -> 492 us (1.13)
  waiting for transfers between devices: 267 us -> 318 us
    psum x1 -> x2, waiting for transfers between devices: 222 us -> 274 us  [create_columns_here(): arr_in = lax.psum(arr_in, no)]
  transfers between devices with their start and end apart: 5 -> 6, of which waited for: 5 -> 6; matrix products, arithmetic and copies ran while one was open for 6% -> 5% of each run, Pallas kernels for 0% -> 0%
where the time goes in v1:
time: 492 us; the launch traced here: 491 us
  waiting for transfers between devices  318 us (65%)
  local copies, waits for them, and re-layouts  43.3 us (9%)
  matrix products  37.4 us (8%)
  starting transfers between devices  27.5 us (6%)
  blocking collectives  26.2 us (5%)
  other arithmetic  23.4 us (5%)
  between operations  14.4 us (3%)
    psum x2, waiting for transfers between devices, create_columns_here(): arr_in = lax.psum(arr_in, no)  274 us
    all_to_all x1, blocking collectives, send_asked(): lax.all_to_all(wanted, 'dp', split_axis=0, concat_axis=0, tiled=True)  18.3 us
    all_to_all x1, waiting for transfers between devices, send_returned(): lax.all_to_all(gradients, 'dp', split_axis=0, concat_axis=0, tiled=True)  17.5 us
    all_to_all x1, waiting for transfers between devices, send_fetched(): lax.all_to_all(fetched, 'dp', split_axis=0, concat_axis=0, tiled=True)  15.3 us
    all_to_all x1, starting transfers between devices, send_returned(): lax.all_to_all(gradients, 'dp', split_axis=0, concat_axis=0, tiled=True)  10.8 us
  transfers between devices with their start and end apart: 6, of which 6 were waited for; matrix products, arithmetic and copies ran while one was open for 5% of the time, Pallas kernels for 0%

profile of v1, /device:TPU:97, one launch (start us, length us, event | category | flops | bytes accessed | tf_op | source)
XLA Modules:
  0.0 490.6 jit_solution(18214806253786493909)
XLA Ops:
  7.2 0.9 reshape.199
  8.2 18.3 %all_to_all.30 = s32[64,4,2]{1,2,0:T(2,128)S(1)} all-to-all(s32[64,4,2]{1,2,0:T(2,128)S(1)} %copy.143), channel_id=1, replica_groups=mesh['dp'=64,'rep'=4] {'dp'}, dimensions={0} | all-to-all | bytes 4096 | tf_op jit(solution)/shard_map/all_to_all | solution.py:69
  26.7 7.9 %all_to_all.31 = s32[4,1,128]{2,1,0:T(1,128)S(1)} all-to-all(s32[4,1,128]{2,1,0:T(1,128)S(1)} %reshape.234), channel_id=1, replica_groups=mesh['dp'=64,'rep'=4] {'rep'}, dimensions={0} | all-to-all | bytes 4096 | tf_op jit(solution)/shard_map/all_to_all | solution.py:68
  34.6 0.5 broadcast.167
  35.1 0.7 reduce.3
  36.2 3.6 gather_fusion
  39.8 2.0 reshape.215
  41.8 8.5 %all-to-all-start.2 = ((bf16[64,4,2,512]{3,2,1,0:T(2,128)(2,1)}), bf16[64,4,2,512]{3,2,1,0:T(2,128)(2,1)S(1)}, u32[]{:S(2)}, u32[]{:S(2)}) async-start(bf16[64,4,2,512]{3,2,1,0:T(2,128)(2,1)} %reshape.215), calls=%async_computation.2 | async-start | bytes 1048576 | tf_op jit(solution)/shard_map/all_to_all | solution.py:80
  50.6 1.0 copy.163
  51.8 15.3 %all-to-all-done.2 = bf16[64,4,2,512]{3,2,1,0:T(2,128)(2,1)S(1)} async-done(((bf16[64,4,2,512]{3,2,1,0:T(2,128)(2,1)}), bf16[64,4,2,512]{3,2,1,0:T(2,128)(2,1)S(1)}, u32[]{:S(2)}, u32[]{:S(2)}) %all-to-all-start.2) | async-done | bytes 524320 | tf_op jit(solution)/shard_map/all_to_all | solution.py:80
  67.1 1.2 copy.146
  68.3 3.5 all-to-all-start.3
  72.2 2.3 fusion.42
  74.5 7.3 %all-to-all-done.3 = bf16[64,4,2,512]{3,2,0,1:T(2,128)(2,1)S(1)} async-done(((bf16[64,4,2,512]{3,2,0,1:T(2,128)(2,1)}), bf16[64,4,2,512]{3,2,0,1:T(2,128)(2,1)S(1)}, u32[]{:S(2)}, u32[]{:S(2)}) %all-to-all-start.3) | async-done | bytes 524320 | tf_op jit(solution)/shard_map/all_to_all | solution.py:79
  81.7 1.2 copy.147
  82.9 2.0 reshape.200
  84.9 2.0 convert_reduce_fusion
  87.2 0.6 copy-done.16
  87.8 3.8 multiply_convert_fusion
  91.6 1.4 copy-done.7
  93.0 1.2 slice_bitcast_fusion
  94.1 2.1 copy.176
  96.2 2.0 copy.177
  98.3 4.9 select_convert_fusion
  103.1 0.8 fusion.41
  104.0 0.9 copy-done.1
  104.9 0.8 fusion.20
  105.7 2.6 copy.171
  108.3 2.1 multiply_reduce_fusion
  110.4 0.7 multiply_multiply_fusion.1
  111.1 3.0 fusion.40
  114.1 0.9 broadcast_add_fusion
  115.0 2.1 copy.172
  117.1 5.1 %fusion.4 = bf16[4,512,512]{2,1,0:T(8,128)(2,1)S(1)} fusion(f32[4,512,512]{2,1,0:T(8,128)} %get-tuple-element.60, pred[512,512]{1,0:T(8,128)(4,1)S(1)} %fusion.22, bf16[4,128,512]{2,1,0:T(8,128)(2,1)} %bitcast.72, bf16[64,4,8,128]{3,2,1,0:T(8,128)(2,1)} %get-tuple-element.49), kind=kOutput, calls=%fused_computation.10 | convolution fusion | flops 283115520 | bytes 7602176 | tf_op jit(solution)/shard_map/transpose(jvp(hqk,khd->qhd))/dot_general | solution.py:54
  122.2 1.2 fusion.45
  123.4 1.6 fusion.44
  125.0 1.5 fusion.43
  126.5 2.1 copy.173
  128.6 2.0 copy.174
  130.6 2.1 copy.175
  132.7 3.6 fusion
  136.3 3.3 fusion.5
  139.6 1.3 fusion.18
  141.6 0.8 copy-done.12
  142.4 1.1 fusion.13
  143.6 1.4 fusion.10
  145.1 119.4 %all-reduce.11.cloned.1.call-done = (f32[256,512]{1,0:T(8,128)}, f32[512,2048]{1,0:T(8,128)}, f32[512,512]{1,0:T(8,128)}) async-done(((f32[256,512]{1,0:T(8,128)}, f32[512,2048]{1,0:T(8,128)}, f32[512,512]{1,0:T(8,128)}), (f32[256,512]{1,0:T(8,128)}, f32[512,2048]{1,0:T(8,128)}, f32[512,512]{1,0:T(8,128)})) %all-reduce.11.cloned.1.call-update) | async-done | bytes 5767184 | tf_op jit(solution)/shard_map/psum | solution.py:124
  264.5 2.5 convolution_convert_fusion.1
  267.1 2.0 reshape.212
  269.1 10.8 %all-to-all-start.4 = ((bf16[64,4,2,512]{3,2,1,0:T(2,128)(2,1)}), bf16[64,4,2,512]{3,2,1,0:T(2,128)(2,1)}, u32[]{:S(2)}, u32[]{:S(2)}) async-start(bf16[64,4,2,512]{3,2,1,0:T(2,128)(2,1)} %reshape.212), calls=%async_computation.4 | async-start | bytes 1048576 | tf_op jit(solution)/shard_map/all_to_all | solution.py:91
  280.3 17.5 %all-to-all-done.4 = bf16[64,4,2,512]{3,2,1,0:T(2,128)(2,1)} async-done(((bf16[64,4,2,512]{3,2,1,0:T(2,128)(2,1)}), bf16[64,4,2,512]{3,2,1,0:T(2,128)(2,1)}, u32[]{:S(2)}, u32[]{:S(2)}) %all-to-all-start.4) | async-done | bytes 524320 | tf_op jit(solution)/shard_map/all_to_all | solution.py:91
  297.7 2.2 copy.164
  299.9 4.4 all-to-all-start.5
  304.3 2.3 fusion.11
  306.7 2.1 copy.167
  308.7 4.1 all-to-all-done.5
  312.9 1.2 copy_convert_fusion
  314.1 1.8 copy.166
  315.9 1.9 reshape.226
  317.8 4.2 scatter_custom_fusion
  322.1 154.9 %all-reduce.9.cloned.1.call-done = (f32[256,512]{1,0:T(8,128)}, f32[512,2048]{1,0:T(8,128)}, f32[512,512]{1,0:T(8,128)}) async-done(((f32[256,512]{1,0:T(8,128)}, f32[512,2048]{1,0:T(8,128)}, f32[512,512]{1,0:T(8,128)}), (f32[256,512]{1,0:T(8,128)}, f32[512,2048]{1,0:T(8,128)}, f32[512,512]{1,0:T(8,128)})) %all-reduce.9.cloned.1.call-update) | async-done | bytes 5767184 | tf_op jit(solution)/shard_map/psum | solution.py:124
  477.0 4.9 %broadcast_multiply_fusion = f32[512,2048]{1,0:T(8,128)} fusion(f32[512,2048]{1,0:T(8,128)} %get-tuple-element.41), kind=kLoop, calls=%fused_computation.17 | loop fusion | flops 1048576 | bytes 8388608 | tf_op jit(solution)/shard_map/mul | solution.py:136
  481.9 1.1 broadcast_multiply_fusion.1
  483.0 0.8 broadcast_multiply_fusion.2
  (70 shorter events, 2.9 us)
Async XLA Ops:
  7.2 80.6 %copy-start = (bf16[512,2048]{1,0:T(8,128)(2,1)S(1)}, bf16[512,2048]{1,0:T(8,128)(2,1)}, u32[]{:S(2)}) copy-start(bf16[512,2048]{1,0:T(8,128)(2,1)} %param.15) | copy-start | bytes 6291460
  7.2 43.2 %copy-start.21 = (s32[1,4]{1,0:T(1,128)S(1)}, s32[1,4]{1,0:T(1,128)}, u32[]{:S(2)}) copy-start(s32[1,4]{1,0:T(1,128)} %param.12) | copy-start | bytes 52
  7.2 43.4 %copy-start.4 = (bf16[512,512]{1,0:T(8,128)(2,1)S(1)}, bf16[512,512]{1,0:T(8,128)(2,1)}, u32[]{:S(2)}) copy-start(bf16[512,512]{1,0:T(8,128)(2,1)} %param.17) | copy-start | bytes 1572868
  26.5 25.1 %copy-start.18 = (s32[512,8]{0,1:T(8,128)S(1)}, s32[512,8]{0,1:T(8,128)}, u32[]{:S(2)}) copy-start(s32[512,8]{0,1:T(8,128)} %param.13) | copy-start | bytes 49156
  41.8 43.1 %copy-start.19 = (s32[512]{0:T(512)S(1)}, s32[512]{0:T(512)}, u32[]{:S(2)}) copy-start(s32[512]{0:T(512)} %param.11) | copy-start | bytes 6148
  41.8 25.3 %all-to-all-start.2 = ((bf16[64,4,2,512]{3,2,1,0:T(2,128)(2,1)}), bf16[64,4,2,512]{3,2,1,0:T(2,128)(2,1)S(1)}, u32[]{:S(2)}, u32[]{:S(2)}) async-start(bf16[64,4,2,512]{3,2,1,0:T(2,128)(2,1)} %reshape.215), calls=%async_computation.2 | async-start | bytes 1048576 | tf_op jit(solution)/shard_map/all_to_all | solution.py:80
  68.3 13.5 %all-to-all-start.3 = ((bf16[64,4,2,512]{3,2,0,1:T(2,128)(2,1)}), bf16[64,4,2,512]{3,2,0,1:T(2,128)(2,1)S(1)}, u32[]{:S(2)}, u32[]{:S(2)}) async-start(bf16[64,4,2,512]{3,2,0,1:T(2,128)(2,1)} %copy.146), calls=%async_computation.3 | async-start | bytes 1048576 | tf_op jit(solution)/shard_map/all_to_all | solution.py:79
  71.7 192.7 %all-reduce.11.cloned.1.call-start = ((), (), s32[]{:S(2)}) async-start(), calls=%async_computation.7 | async-start | bytes 11534336 | tf_op jit(solution)/shard_map/psum | solution.py:124
  87.2 0.6 copy-start.16
  91.6 1.4 copy-start.7
  98.3 4.9 copy-start.8
  103.1 2.6 copy-start.2
  104.0 1.0 copy-start.1
  117.1 5.1 %copy-start.10 = (bf16[512,512]{0,1:T(8,128)(2,1)S(1)}, bf16[512,512]{0,1:T(8,128)(2,1)}, u32[]{:S(2)}) copy-start(bf16[512,512]{0,1:T(8,128)(2,1)} %copy.176) | copy-start | bytes 1572868
  117.1 6.3 %copy-start.11 = (bf16[512,512]{0,1:T(8,128)(2,1)S(1)}, bf16[512,512]{0,1:T(8,128)(2,1)}, u32[]{:S(2)}) copy-start(bf16[512,512]{0,1:T(8,128)(2,1)} %copy.177) | copy-start | bytes 1572868
  122.1 2.9 copy-start.3
  122.2 2.9 copy-start.13
  139.6 1.3 copy-start.17
  139.6 1.6 copy-start.9
  139.6 3.9 copy-start.5
  141.6 0.8 copy-start.12
  145.0 119.5 %copy-start.20 = (s32[512]{0:T(512)S(1)}, s32[512]{0:T(512)}, u32[]{:S(2)}) copy-start(s32[512]{0:T(512)} %param.11) | copy-start | bytes 6148
  145.0 331.9 %all-reduce.9.cloned.1.call-start = ((), (), s32[]{:S(2)}) async-start(), calls=%async_computation.6 | async-start | bytes 11534336 | tf_op jit(solution)/shard_map/psum | solution.py:124
  264.5 39.8 %copy-start.6 = (bf16[512,512]{1,0:T(8,128)(2,1)S(1)}, bf16[512,512]{1,0:T(8,128)(2,1)}, u32[]{:S(2)}) copy-start(bf16[512,512]{1,0:T(8,128)(2,1)} %get-tuple-element.48) | copy-start | bytes 1572868
  269.1 28.6 %all-to-all-start.4 = ((bf16[64,4,2,512]{3,2,1,0:T(2,128)(2,1)}), bf16[64,4,2,512]{3,2,1,0:T(2,128)(2,1)}, u32[]{:S(2)}, u32[]{:S(2)}) async-start(bf16[64,4,2,512]{3,2,1,0:T(2,128)(2,1)} %reshape.212), calls=%async_computation.4 | async-start | bytes 1048576 | tf_op jit(solution)/shard_map/all_to_all | solution.py:91
  299.9 13.0 %all-to-all-start.5 = ((bf16[64,4,2,512]{3,2,0,1:T(2,128)(2,1)}), bf16[64,4,2,512]{3,2,0,1:T(2,128)(2,1)}, u32[]{:S(2)}, u32[]{:S(2)}) async-start(bf16[64,4,2,512]{3,2,0,1:T(2,128)(2,1)} %copy.164), calls=%async_computation.5 | async-start | bytes 1048576 | tf_op jit(solution)/shard_map/all_to_all | solution.py:90
  477.0 4.9 %copy-start.14 = (f32[512,512]{1,0:T(8,128)S(1)}, f32[512,512]{1,0:T(8,128)}, u32[]{:S(2)}) copy-start(f32[512,512]{1,0:T(8,128)} %get-tuple-element.42) | copy-start | bytes 3145732
  477.0 6.0 %copy-start.15 = (f32[256,512]{1,0:T(8,128)S(1)}, f32[256,512]{1,0:T(8,128)}, u32[]{:S(2)}) copy-start(f32[256,512]{1,0:T(8,128)} %get-tuple-element.40) | copy-start | bytes 1572868
Sparse Core Ops, SparseCore 0:
  145.2 119.2 all-reduce.10
  268.4 208.5 all-reduce.8
